TPU v7x, 1024 devices: a whole 4x4x32 slice. The times are simulated.
1024 devices in a mesh: gx: 16 (over z_lo), gy: 8 (over z_hi, y), gz: 8 (over x, core).
Axes of the slice: x: 4, y: 4, z: 32 (z_hi: 2, z_lo: 16; z = z_hi * 16 + z_lo), core: 2. Of those that a mesh axis runs over, the one named last changes fastest.
Arguments:
- state: float32 [9, 256, 128, 1024], P(None, 'gx', 'gy', 'gz'), may hold values from 0 to 1
- mobility: float32 [8], replicated, may hold values from 0.5 to 2
- seeds: int32 [2, 2, 256, 128], replicated, may hold values from 0 to 8
- frame_shifts: int32 [2], replicated, may hold values from 0 to 2, as said below
Outputs:
- state_out: float32 [9, 256, 128, 1024], P(None, 'gx', 'gy', 'gz')
Inputs may be any that keep to these rules, and one draw needn't show every extreme that they name: A value of 8 seeds no grain in that cell. `frame_shifts`: the frame advances 2 planes in at least one step and stays in place in at least one other.
All inputs are finite; a program needn't handle non-finite values.
Results may differ from a plain program's by a relative error of at most 0.0001.
Values sent between devices are 32-bit elements; how exact they have to be, the bound alone decides.
A program may use at most 32 MiB of HBM per device.

v0:
```python
import jax
import jax.numpy as jnp
from jax import lax
from jax.sharding import PartitionSpec as P

step_rate = 0.1
stiffness = 0.7
coupling = 0.5
diffusion = 0.14
rejection = 0.5
nucleus = 0.3
melt_solute = 1.0


def extended(block, sides, width):
    for axis, dim in sides:
        count = lax.axis_size(axis)
        forward = [(i, i + 1) for i in range(count - 1)]
        backward = [(target, source) for source, target in forward]
        low = lax.ppermute(
            lax.slice_in_dim(block, block.shape[dim] - width, None, axis=dim), axis, forward
        )
        high = lax.ppermute(lax.slice_in_dim(block, 0, width, axis=dim), axis, backward)
        block = jnp.concatenate([low, block, high], axis=dim)
    return block


def padded_2(value, sides, width):
    edges = {}
    for axis, dim in sides:
        count, length = (lax.axis_size(axis), value.shape[dim])
        up = [(i, (i + 1) % count) for i in range(count)]
        last = lax.slice_in_dim(value, length - width, length, axis=dim)
        first = lax.slice_in_dim(value, 0, width, axis=dim)
        edges[dim] = (
            lax.ppermute(last, axis, up),
            lax.ppermute(first, axis, [(b, a) for a, b in up]),
        )
    done = []
    for _, dim in sides:
        low, high = edges[dim]
        around = [(width, width) if d in done else (0, 0) for d in range(value.ndim)]
        value = jnp.concatenate([jnp.pad(low, around), value, jnp.pad(high, around)], axis=dim)
        done.append(dim)
    return value


def entering_planes(seeds, step, margin, width_x, width_y, grains):
    total_x = seeds.shape[2]
    total_y = seeds.shape[3]
    rows = (
        lax.axis_index("gx") * (width_x - 2 * margin)
        - margin
        + jnp.arange(width_x, dtype=jnp.int32)
    ) % total_x
    cols = (
        lax.axis_index("gy") * (width_y - 2 * margin)
        - margin
        + jnp.arange(width_y, dtype=jnp.int32)
    ) % total_y
    marks = jnp.take(jnp.take(seeds[step], rows, axis=1), cols, axis=2)
    marks = jnp.transpose(marks, (1, 2, 0))
    labels = jnp.arange(grains, dtype=jnp.int32)
    nuclei = nucleus * (marks[None] == labels[:, None, None, None]).astype(jnp.float32)
    melt = jnp.full((1, width_x, width_y, seeds.shape[1]), melt_solute, jnp.float32)
    return jnp.concatenate([nuclei, melt], axis=0)


def frame_section(field, count, seeds, step, margin):
    grains = field.shape[0] - 1
    depth = seeds.shape[1]
    length = field.shape[3]
    entering = entering_planes(seeds, step, margin, field.shape[1], field.shape[2], grains)
    topmost = lax.axis_index("gz") == lax.axis_size("gz") - 1
    lowest = lax.axis_index("gz") == 0
    padded = extended(field, (("gz", 3),), depth + 1)
    blank = jnp.zeros(entering.shape[:3] + (1,), jnp.float32)
    filler = jnp.concatenate([entering, blank], axis=3)
    planes = jnp.arange(depth + 1, dtype=jnp.int32)
    filler = jnp.where(planes < count, filler, 0.0)
    upper = jnp.where(topmost, filler, padded[:, :, :, length + depth + 1 :])
    padded = jnp.concatenate([padded[:, :, :, : length + depth + 1], upper], axis=3)
    tall = lax.dynamic_slice_in_dim(padded, count + depth, length + 2, axis=3)
    bottom = jnp.where(lowest, 0.0, tall[:, :, :, :1])
    tall = jnp.concatenate([bottom, tall[:, :, :, 1:]], axis=3)
    return tall


def update(wide, tall, mobility):
    grains = tall.shape[0] - 1
    length = tall.shape[3] - 2
    center = tall[:, :, :, 1:-1]
    beside = wide[:, :-2, 1:-1] + wide[:, 2:, 1:-1] + wide[:, 1:-1, :-2] + wide[:, 1:-1, 2:]
    beside = beside + tall[:, :, :, :-2] + tall[:, :, :, 2:]
    lap = beside - 6.0 * center
    phases = center[:grains]
    solute = center[grains]
    squares = jnp.sum(phases * phases, axis=0)
    depth_all = length * lax.axis_size("gz")
    zpos = (lax.axis_index("gz") * length).astype(jnp.float32) + jnp.arange(
        length, dtype=jnp.float32
    )
    theta = 1.0 - 2.0 * (zpos + 0.5) / depth_all
    alpha = theta - coupling * solute
    drive = -alpha * phases + phases * phases * phases + phases * (squares - phases * phases)
    fresh = phases + step_rate * mobility[:, None, None, None] * (stiffness * lap[:grains] - drive)
    squares_new = jnp.sum(fresh * fresh, axis=0)
    solute_new = solute + diffusion * lap[grains] - rejection * solute * (squares_new - squares)
    return jnp.concatenate([fresh, solute_new[None]], axis=0)


def shards(state, mobility, seeds, frame_shifts):
    field = state
    total_steps = frame_shifts.shape[0]
    for step in range(total_steps):
        tall = frame_section(field, frame_shifts[step], seeds, step, 0)
        wide = padded_2(tall[:, :, :, 1:-1], (("gx", 1), ("gy", 2)), 1)
        field = update(wide, tall, mobility)
    return field


def solution(mesh):
    placed = (P(None, "gx", "gy", "gz"), P(), P(), P())
    return jax.shard_map(
        shards, mesh=mesh, in_specs=placed, out_specs=P(None, "gx", "gy", "gz"), check_vma=False
    )
```

profile of v0, /device:TPU:6, one launch (start us, length us, event | category | flops | bytes accessed | tf_op | source)
XLA Modules:
  0.0 158.6 jit_solution(8152508816829375794)
XLA Ops:
  0.0 2.1 %fusion.36 = (f32[9,16,16,3]{3,2,1,0:T(8,128)S(1)}, f32[9,16,16,3]{3,2,1,0:T(8,128)S(1)}) fusion(f32[9,16,16,128]{3,2,1,0:T(8,128)} %param.8), kind=kLoop, calls=%fused_computation.111 | loop fusion | bytes 110592 | tf_op jit(solution)/shard_map/slice | solution.py:21
  2.1 1.0 copy.53
  3.1 2.2 %collective-permute-start.1 = (f32[9,16,16,3]{2,1,3,0:T(8,128)S(1)}, f32[9,16,16,3]{2,1,3,0:T(8,128)S(1)}, u32[]{:S(2)}, u32[]{:S(2)}) collective-permute-start(f32[9,16,16,3]{2,1,3,0:T(8,128)S(1)} %copy.53), channel_id=1, source_target_pairs={{1,0},{2,1},{3,2},{4,3},{5,4},{6,5},{7,6},{9,8},{10,9},{11,10},{12... | collective-permute-start | bytes 82952 | tf_op jit(solution)/shard_map/ppermute | solution.py:23
  5.2 1.0 copy.51
  6.2 2.2 %collective-permute-start = (f32[9,16,16,3]{2,1,3,0:T(8,128)S(1)}, f32[9,16,16,3]{2,1,3,0:T(8,128)}, u32[]{:S(2)}, u32[]{:S(2)}) collective-permute-start(f32[9,16,16,3]{2,1,3,0:T(8,128)S(1)} %copy.51), channel_id=1, source_target_pairs={{0,1},{1,2},{2,3},{3,4},{4,5},{5,6},{6,7},{8,9},{9,10},{10,11},{11... | collective-permute-start | bytes 82952 | tf_op jit(solution)/shard_map/ppermute | solution.py:20
  16.2 1.8 %copy.34 = f32[9,16,16,3]{3,2,1,0:T(8,128)S(1)} copy(f32[9,16,16,3]{2,1,3,0:T(8,128)} %collective-permute-done) | data formatting | bytes 55296 | tf_op jit(solution)/shard_map/ppermute | solution.py:20
  18.1 1.6 %dynamic-slice_maximum_fusion.3 = f32[9,16,16,130]{3,2,1,0:T(8,128)S(1)} fusion(s32[]{:T(128)S(6)} %select_n.70, f32[9,16,16,3]{3,2,1,0:T(8,128)S(1)} %copy.35, f32[9,16,16,128]{3,2,1,0:T(8,128)S(1)} %copy-done, f32[9,16,16,3]{3,2,1,0:T(8,128)S(1)} %copy.34), kind=kLoop, calls=%fused_computation.7 | loop fusion | flops 599040 | bytes 2433028 | tf_op jit(solution)/shard_map/concatenate | solution.py:82
  20.3 3.5 %collective-permute-start.4 = (f32[9,16,1,128]{3,1,2,0:T(8,128)S(1)}, f32[9,16,1,128]{3,1,2,0:T(8,128)S(1)}, u32[]{:S(2)}, u32[]{:S(2)}) collective-permute-start(f32[9,16,1,128]{3,1,2,0:T(8,128)S(1)} %bitcast.44), channel_id=1, source_target_pairs={{0,8},{8,16},{16,24},{24,32},{32,40},{40,48},{48,56},{56,0},{1,9},... | collective-permute-start | bytes 221192 | tf_op jit(solution)/shard_map/ppermute | solution.py:36
  23.8 29.9 %collective-permute-start.5 = (f32[9,16,1,128]{3,1,2,0:T(8,128)S(1)}, f32[9,16,1,128]{3,1,2,0:T(8,128)S(1)}, u32[]{:S(2)}, u32[]{:S(2)}) collective-permute-start(f32[9,16,1,128]{3,1,2,0:T(8,128)S(1)} %bitcast.42), channel_id=1, source_target_pairs={{8,0},{16,8},{24,16},{32,24},{40,32},{48,40},{56,48},{0,56},{9,1},... | collective-permute-start | bytes 221192 | tf_op jit(solution)/shard_map/ppermute | solution.py:37
  53.6 2.9 %collective-permute-start.2 = (f32[9,1,16,128]{3,2,1,0:T(8,128)S(1)}, f32[9,1,16,128]{3,2,1,0:T(8,128)S(1)}, u32[]{:S(2)}, u32[]{:S(2)}) collective-permute-start(f32[9,1,16,128]{3,2,1,0:T(8,128)S(1)} %get-tuple-element.17), channel_id=1, source_target_pairs={{0,64},{64,128},{128,192},{192,256},{256,320},{320,384},{384,448},... | collective-permute-start | bytes 221192 | tf_op jit(solution)/shard_map/ppermute | solution.py:36
  56.6 19.1 %collective-permute-start.3 = (f32[9,1,16,128]{3,2,1,0:T(8,128)S(1)}, f32[9,1,16,128]{3,2,1,0:T(8,128)S(1)}, u32[]{:S(2)}, u32[]{:S(2)}) collective-permute-start(f32[9,1,16,128]{3,2,1,0:T(8,128)S(1)} %get-tuple-element.18), channel_id=1, source_target_pairs={{64,0},{128,64},{192,128},{256,192},{320,256},{384,320},{448,384},... | collective-permute-start | bytes 221192 | tf_op jit(solution)/shard_map/ppermute | solution.py:37
  77.2 5.5 %collective-permute-done.2 = f32[9,1,16,128]{3,2,1,0:T(8,128)S(1)} collective-permute-done((f32[9,1,16,128]{3,2,1,0:T(8,128)S(1)}, f32[9,1,16,128]{3,2,1,0:T(8,128)S(1)}, u32[]{:S(2)}, u32[]{:S(2)}) %collective-permute-start.2) | collective-permute-done | bytes 73760 | tf_op jit(solution)/shard_map/ppermute | solution.py:36
  84.7 1.7 %copy.44 = f32[9,16,16,3]{2,1,3,0:T(8,128)} copy(f32[9,16,16,3]{3,2,1,0:T(8,128)S(1)} %get-tuple-element.20) | data formatting | bytes 55296 | tf_op jit(solution)/shard_map/slice | solution.py:23
  86.4 4.4 %collective-permute-start.7 = (f32[9,16,16,3]{2,1,3,0:T(8,128)}, f32[9,16,16,3]{2,1,3,0:T(8,128)S(1)}, u32[]{:S(2)}, u32[]{:S(2)}) collective-permute-start(f32[9,16,16,3]{2,1,3,0:T(8,128)} %copy.44), channel_id=1, source_target_pairs={{1,0},{2,1},{3,2},{4,3},{5,4},{6,5},{7,6},{9,8},{10,9},{11,10},{12... | collective-permute-start | bytes 82952 | tf_op jit(solution)/shard_map/ppermute | solution.py:23
  92.6 1.0 copy.40
  93.6 2.1 %collective-permute-start.6 = (f32[9,16,16,3]{2,1,3,0:T(8,128)S(1)}, f32[9,16,16,3]{2,1,3,0:T(8,128)}, u32[]{:S(2)}, u32[]{:S(2)}) collective-permute-start(f32[9,16,16,3]{2,1,3,0:T(8,128)S(1)} %copy.40), channel_id=1, source_target_pairs={{0,1},{1,2},{2,3},{3,4},{4,5},{5,6},{6,7},{8,9},{9,10},{10,11},{11... | collective-permute-start | bytes 82952 | tf_op jit(solution)/shard_map/ppermute | solution.py:20
  96.7 4.2 %collective-permute-done.6 = f32[9,16,16,3]{2,1,3,0:T(8,128)} collective-permute-done((f32[9,16,16,3]{2,1,3,0:T(8,128)S(1)}, f32[9,16,16,3]{2,1,3,0:T(8,128)}, u32[]{:S(2)}, u32[]{:S(2)}) %collective-permute-start.6) | collective-permute-done | bytes 27680 | tf_op jit(solution)/shard_map/ppermute | solution.py:20
  100.9 1.8 %copy.45 = f32[9,16,16,3]{3,2,1,0:T(8,128)S(1)} copy(f32[9,16,16,3]{2,1,3,0:T(8,128)} %collective-permute-done.6) | data formatting | bytes 55296 | tf_op jit(solution)/shard_map/ppermute | solution.py:20
  102.8 2.1 %dynamic-slice_maximum_fusion = f32[9,16,16,130]{3,2,1,0:T(8,128)S(1)} fusion(s32[]{:T(128)S(6)} %select_n.75, f32[9,16,16,3]{3,2,1,0:T(8,128)S(1)} %copy.46, f32[1,16,16,128]{3,2,1,0:T(8,128)S(1)} %fusion.25, f32[8,16,16,128]{3,2,1,0:T(8,128)S(1)} %get-tuple-element.10, f32[9,16,16,3]{3,2,1,0:T(8,128)S(1)} %copy.45), kind=kLoop, calls=%fused_computation.4 | loop fusion | flops 898560 | bytes 2433028 | tf_op jit(solution)/shard_map/concatenate | solution.py:82
  105.6 1.9 %collective-permute-start.10 = (f32[9,16,1,128]{3,1,2,0:T(8,128)S(1)}, f32[9,16,1,128]{3,1,2,0:T(8,128)S(1)}, u32[]{:S(2)}, u32[]{:S(2)}) collective-permute-start(f32[9,16,1,128]{3,1,2,0:T(8,128)S(1)} %bitcast.45), channel_id=1, source_target_pairs={{0,8},{8,16},{16,24},{24,32},{32,40},{40,48},{48,56},{56,0},{1,9},... | collective-permute-start | bytes 221192 | tf_op jit(solution)/shard_map/ppermute | solution.py:36
  107.5 24.4 %collective-permute-start.11 = (f32[9,16,1,128]{3,1,2,0:T(8,128)S(1)}, f32[9,16,1,128]{3,1,2,0:T(8,128)S(1)}, u32[]{:S(2)}, u32[]{:S(2)}) collective-permute-start(f32[9,16,1,128]{3,1,2,0:T(8,128)S(1)} %bitcast.43), channel_id=1, source_target_pairs={{8,0},{16,8},{24,16},{32,24},{40,32},{48,40},{56,48},{0,56},{9,1},... | collective-permute-start | bytes 221192 | tf_op jit(solution)/shard_map/ppermute | solution.py:37
  131.9 1.9 %collective-permute-start.8 = (f32[9,1,16,128]{3,2,1,0:T(8,128)S(1)}, f32[9,1,16,128]{3,2,1,0:T(8,128)S(1)}, u32[]{:S(2)}, u32[]{:S(2)}) collective-permute-start(f32[9,1,16,128]{3,2,1,0:T(8,128)S(1)} %get-tuple-element.13), channel_id=1, source_target_pairs={{0,64},{64,128},{128,192},{192,256},{256,320},{320,384},{384,448},... | collective-permute-start | bytes 221192 | tf_op jit(solution)/shard_map/ppermute | solution.py:36
  133.8 20.1 %collective-permute-start.9 = (f32[9,1,16,128]{3,2,1,0:T(8,128)S(1)}, f32[9,1,16,128]{3,2,1,0:T(8,128)S(1)}, u32[]{:S(2)}, u32[]{:S(2)}) collective-permute-start(f32[9,1,16,128]{3,2,1,0:T(8,128)S(1)} %get-tuple-element.14), channel_id=1, source_target_pairs={{64,0},{128,64},{192,128},{256,192},{320,256},{384,320},{448,384},... | collective-permute-start | bytes 221192 | tf_op jit(solution)/shard_map/ppermute | solution.py:37
  157.5 1.1 pad_maximum_fusion.15
  (68 shorter events, 16.2 us)
Async XLA Ops:
  2.1 6.4 %copy-start.1 = (s32[2,2,256,128]{3,2,1,0:T(8,128)S(1)}, s32[2,2,256,128]{3,2,1,0:T(8,128)}, u32[]{:S(2)}) copy-start(s32[2,2,256,128]{3,2,1,0:T(8,128)} %param.10) | copy-start | bytes 1572868
  3.1 12.1 %collective-permute-start.1 = (f32[9,16,16,3]{2,1,3,0:T(8,128)S(1)}, f32[9,16,16,3]{2,1,3,0:T(8,128)S(1)}, u32[]{:S(2)}, u32[]{:S(2)}) collective-permute-start(f32[9,16,16,3]{2,1,3,0:T(8,128)S(1)} %copy.53), channel_id=1, source_target_pairs={{1,0},{2,1},{3,2},{4,3},{5,4},{6,5},{7,6},{9,8},{10,9},{11,10},{12... | collective-permute-start | bytes 82952 | tf_op jit(solution)/shard_map/ppermute | solution.py:23
  6.2 10.0 %collective-permute-start = (f32[9,16,16,3]{2,1,3,0:T(8,128)S(1)}, f32[9,16,16,3]{2,1,3,0:T(8,128)}, u32[]{:S(2)}, u32[]{:S(2)}) collective-permute-start(f32[9,16,16,3]{2,1,3,0:T(8,128)S(1)} %copy.51), channel_id=1, source_target_pairs={{0,1},{1,2},{2,3},{3,4},{4,5},{5,6},{6,7},{8,9},{9,10},{10,11},{11... | collective-permute-start | bytes 82952 | tf_op jit(solution)/shard_map/ppermute | solution.py:20
  8.5 3.4 %copy-start.3 = (s32[2]{0:T(128)S(1)}, s32[2]{0:T(128)}, u32[]{:S(2)}) copy-start(s32[2]{0:T(128)} %param.11) | copy-start | bytes 28
  8.5 4.6 %copy-start.4 = (f32[8]{0:T(128)S(1)}, f32[8]{0:T(128)}, u32[]{:S(2)}) copy-start(f32[8]{0:T(128)} %param.9) | copy-start | bytes 100
  15.3 2.8 %copy-start = (f32[9,16,16,128]{3,2,1,0:T(8,128)S(1)}, f32[9,16,16,128]{3,2,1,0:T(8,128)}, u32[]{:S(2)}) copy-start(f32[9,16,16,128]{3,2,1,0:T(8,128)} %param.8) | copy-start | bytes 3538948
  20.3 56.9 %collective-permute-start.4 = (f32[9,16,1,128]{3,1,2,0:T(8,128)S(1)}, f32[9,16,1,128]{3,1,2,0:T(8,128)S(1)}, u32[]{:S(2)}, u32[]{:S(2)}) collective-permute-start(f32[9,16,1,128]{3,1,2,0:T(8,128)S(1)} %bitcast.44), channel_id=1, source_target_pairs={{0,8},{8,16},{16,24},{24,32},{32,40},{40,48},{48,56},{56,0},{1,9},... | collective-permute-start | bytes 221192 | tf_op jit(solution)/shard_map/ppermute | solution.py:36
  23.8 53.4 %collective-permute-start.5 = (f32[9,16,1,128]{3,1,2,0:T(8,128)S(1)}, f32[9,16,1,128]{3,1,2,0:T(8,128)S(1)}, u32[]{:S(2)}, u32[]{:S(2)}) collective-permute-start(f32[9,16,1,128]{3,1,2,0:T(8,128)S(1)} %bitcast.42), channel_id=1, source_target_pairs={{8,0},{16,8},{24,16},{32,24},{40,32},{48,40},{56,48},{0,56},{9,1},... | collective-permute-start | bytes 221192 | tf_op jit(solution)/shard_map/ppermute | solution.py:37
  53.6 29.1 %collective-permute-start.2 = (f32[9,1,16,128]{3,2,1,0:T(8,128)S(1)}, f32[9,1,16,128]{3,2,1,0:T(8,128)S(1)}, u32[]{:S(2)}, u32[]{:S(2)}) collective-permute-start(f32[9,1,16,128]{3,2,1,0:T(8,128)S(1)} %get-tuple-element.17), channel_id=1, source_target_pairs={{0,64},{64,128},{128,192},{192,256},{256,320},{320,384},{384,448},... | collective-permute-start | bytes 221192 | tf_op jit(solution)/shard_map/ppermute | solution.py:36
  56.6 26.2 %collective-permute-start.3 = (f32[9,1,16,128]{3,2,1,0:T(8,128)S(1)}, f32[9,1,16,128]{3,2,1,0:T(8,128)S(1)}, u32[]{:S(2)}, u32[]{:S(2)}) collective-permute-start(f32[9,1,16,128]{3,2,1,0:T(8,128)S(1)} %get-tuple-element.18), channel_id=1, source_target_pairs={{64,0},{128,64},{192,128},{256,192},{320,256},{384,320},{448,384},... | collective-permute-start | bytes 221192 | tf_op jit(solution)/shard_map/ppermute | solution.py:37
  86.4 9.3 %copy-start.2 = (f32[8,16,16,2]{2,1,3,0:T(8,128)S(1)}, f32[8,16,16,2]{2,1,3,0:T(8,128)}, u32[]{:S(2)}) copy-start(f32[8,16,16,2]{2,1,3,0:T(8,128)} %fusion.27) | copy-start | bytes 49156
  86.4 9.3 %collective-permute-start.7 = (f32[9,16,16,3]{2,1,3,0:T(8,128)}, f32[9,16,16,3]{2,1,3,0:T(8,128)S(1)}, u32[]{:S(2)}, u32[]{:S(2)}) collective-permute-start(f32[9,16,16,3]{2,1,3,0:T(8,128)} %copy.44), channel_id=1, source_target_pairs={{1,0},{2,1},{3,2},{4,3},{5,4},{6,5},{7,6},{9,8},{10,9},{11,10},{12... | collective-permute-start | bytes 82952 | tf_op jit(solution)/shard_map/ppermute | solution.py:23
  93.6 7.4 %collective-permute-start.6 = (f32[9,16,16,3]{2,1,3,0:T(8,128)S(1)}, f32[9,16,16,3]{2,1,3,0:T(8,128)}, u32[]{:S(2)}, u32[]{:S(2)}) collective-permute-start(f32[9,16,16,3]{2,1,3,0:T(8,128)S(1)} %copy.40), channel_id=1, source_target_pairs={{0,1},{1,2},{2,3},{3,4},{4,5},{5,6},{6,7},{8,9},{9,10},{10,11},{11... | collective-permute-start | bytes 82952 | tf_op jit(solution)/shard_map/ppermute | solution.py:20
  105.6 49.8 %collective-permute-start.10 = (f32[9,16,1,128]{3,1,2,0:T(8,128)S(1)}, f32[9,16,1,128]{3,1,2,0:T(8,128)S(1)}, u32[]{:S(2)}, u32[]{:S(2)}) collective-permute-start(f32[9,16,1,128]{3,1,2,0:T(8,128)S(1)} %bitcast.45), channel_id=1, source_target_pairs={{0,8},{8,16},{16,24},{24,32},{32,40},{40,48},{48,56},{56,0},{1,9},... | collective-permute-start | bytes 221192 | tf_op jit(solution)/shard_map/ppermute | solution.py:36
  107.5 47.8 %collective-permute-start.11 = (f32[9,16,1,128]{3,1,2,0:T(8,128)S(1)}, f32[9,16,1,128]{3,1,2,0:T(8,128)S(1)}, u32[]{:S(2)}, u32[]{:S(2)}) collective-permute-start(f32[9,16,1,128]{3,1,2,0:T(8,128)S(1)} %bitcast.43), channel_id=1, source_target_pairs={{8,0},{16,8},{24,16},{32,24},{40,32},{48,40},{56,48},{0,56},{9,1},... | collective-permute-start | bytes 221192 | tf_op jit(solution)/shard_map/ppermute | solution.py:37
  131.9 23.5 %collective-permute-start.8 = (f32[9,1,16,128]{3,2,1,0:T(8,128)S(1)}, f32[9,1,16,128]{3,2,1,0:T(8,128)S(1)}, u32[]{:S(2)}, u32[]{:S(2)}) collective-permute-start(f32[9,1,16,128]{3,2,1,0:T(8,128)S(1)} %get-tuple-element.13), channel_id=1, source_target_pairs={{0,64},{64,128},{128,192},{192,256},{256,320},{320,384},{384,448},... | collective-permute-start | bytes 221192 | tf_op jit(solution)/shard_map/ppermute | solution.py:36
  133.8 22.1 %collective-permute-start.9 = (f32[9,1,16,128]{3,2,1,0:T(8,128)S(1)}, f32[9,1,16,128]{3,2,1,0:T(8,128)S(1)}, u32[]{:S(2)}, u32[]{:S(2)}) collective-permute-start(f32[9,1,16,128]{3,2,1,0:T(8,128)S(1)} %get-tuple-element.14), channel_id=1, source_target_pairs={{64,0},{128,64},{192,128},{256,192},{320,256},{384,320},{448,384},... | collective-permute-start | bytes 221192 | tf_op jit(solution)/shard_map/ppermute | solution.py:37
where the time goes:
time: 159 us
  starting transfers between devices  115 us (72%)
  local copies, waits for them, and re-layouts  19 us (12%)
  other arithmetic  11.7 us (7%)
  waiting for transfers between devices  10.3 us (6%)
  between operations  2.9 us (2%)
    ppermute x4, starting transfers between devices, padded_2(): lax.ppermute(first, axis, [(b, a) for a, b in up])  93.5 us
    ppermute x4, starting transfers between devices, padded_2(): lax.ppermute(last, axis, up)  10.3 us
    ppermute x2, starting transfers between devices, extended(): lax.ppermute(lax.slice_in_dim(block, 0, width, axis=dim), axis, backward)  6.63 us
    ppermute x4, waiting for transfers between devices, padded_2(): lax.ppermute(last, axis, up)  5.51 us
    ppermute x2, starting transfers between devices, extended(): lax.ppermute(lax.slice_in_dim(block, block.shape[dim] - width, None, axis...  4.27 us
    ppermute x2, waiting for transfers between devices, extended(): lax.ppermute(lax.slice_in_dim(block, block.shape[dim] - width, None, axis...  4.23 us
    ppermute x2, local copies, waits for them, and re-layouts, extended(): lax.ppermute(lax.slice_in_dim(block, block.shape[dim] - width, None, axis...  3.68 us
    concatenate x2, other arithmetic, frame_section(): jnp.concatenate([padded[:, :, :, :length + depth + 1], upper], axis=3)  3.65 us
  transfers between devices with their start and end apart: 12, of which 3 were waited for; matrix products, arithmetic and copies ran while one was open for 8% of the time, Pallas kernels for 0%

commit v1 on v0

v1 whole, which is shorter than its diff:
```python
import functools

import jax
import jax.numpy as jnp
from jax import lax
from jax.experimental import pallas as pl
from jax.experimental.pallas import tpu as pltpu
from jax.sharding import PartitionSpec as P

step_rate = 0.1
stiffness = 0.7
coupling = 0.5
diffusion = 0.14
rejection = 0.5
nucleus = 0.3
melt_solute = 1.0

MESH = pl.DeviceIdType.MESH
FIELDS = 9
GRAINS = 8
W = 16
COLUMN = 4
f32 = jnp.float32


def iota(shape, dim):
    return lax.broadcasted_iota(jnp.int32, shape, dim)


def kernel(sizes, mob, shifts, state, seeds, out, F0, F1, H0, H1, relay, pack, packed, xl, xr, xlh, xrh, eh,
           E0m, E0h, E1m, E1h, E2m, marks, seedbuf, local, send, recv):
    nx, ny, nz = sizes
    gx, gy, gz = lax.axis_index("gx"), lax.axis_index("gy"), lax.axis_index("gz")
    col = lax.rem(gy, COLUMN)

    def at(dx, dy, dz=0):
        return (lax.rem(gx + dx + nx, nx), lax.rem(gy + dy + ny, ny), lax.rem(gz + dz + nz, nz))

    far = at(0, jnp.where(col >= 2, 2, -2))
    around = [at(1, 0), at(-1, 0), at(0, 1), at(0, -1), at(1, 1), at(1, -1), at(-1, 1), at(-1, -1)]
    partners = around + [at(0, 0, 1), at(0, 0, -1), far]

    barrier = pltpu.get_barrier_semaphore()
    for partner in partners:
        pl.semaphore_signal(barrier, inc=1, device_id=partner, device_id_type=MESH)

    own = [
        pltpu.make_async_copy(state, F0.at[:, 2:18], local.at[0]),
        pltpu.make_async_copy(state.at[:, :, 0:1], H0.at[:, 2:18, 2:3], local.at[1]),
        pltpu.make_async_copy(state.at[:, :, 15:16], H0.at[:, 2:18, 4:5], local.at[2]),
        pltpu.make_async_copy(seeds, seedbuf, local.at[3]),
    ]
    for copy in own:
        copy.start()

    lane = iota((8, 128), 1)
    row = iota((8, 128), 0)
    group = lane // 6
    spot = lane - 6 * group

    own[0].wait()
    for f in range(FIELDS):
        for t in range(2):
            rows = slice(8 * t, 8 * t + 8)
            acc = jnp.zeros((8, 128), f32)
            for x in range(W):
                moved = pltpu.roll(F0[f, x + 2, rows], 6 * (x + 2) + 2, 1)
                acc = jnp.where((group == x + 2) & (spot >= 2), moved, acc)
            pack[f, rows] = acc
    for t in range(2):
        rows = slice(8 * t, 8 * t + 8)
        low = jnp.zeros((8, 128), f32)
        high = jnp.zeros((8, 128), f32)
        for f in range(FIELDS):
            acc = pack[f, rows]
            here = lane // 12 == f
            low = jnp.where(here, pltpu.roll(acc, (12 * f - 12) % 128, 1), low)
            high = jnp.where(here, pltpu.roll(acc, (12 * f - 96) % 128, 1), high)
        pack[FIELDS, rows] = low
        pack[FIELDS + 1, rows] = high

    pl.semaphore_wait(barrier, len(partners))

    def remote(src, dst, s, r, device):
        return pltpu.make_async_remote_copy(
            src_ref=src, dst_ref=dst, send_sem=send.at[s], recv_sem=recv.at[r], device_id=device, device_id_type=MESH
        )

    A, B = slice(0, 8), slice(8, 16)
    hA, hB = slice(2, 10), slice(10, 18)
    top, bottom = slice(14, 16), slice(0, 2)
    up_a = remote(state.at[:, A, top], H0.at[:, hA, 0:2], 0, 0, at(0, 1))
    up_b = remote(state.at[:, B, top], H0.at[:, hB, 0:2], 1, 1, at(0, 1))
    down_a = remote(state.at[:, A, bottom], H0.at[:, hA, 5:7], 2, 2, at(0, -1))
    down_b = remote(state.at[:, B, bottom], H0.at[:, hB, 5:7], 3, 3, at(0, -1))
    up_r = remote(state.at[:, B, top], relay, 1, 4, at(0, -1))
    down_r = remote(state.at[:, B, bottom], relay, 3, 4, at(0, 1))
    on_up = remote(relay, H0.at[:, hB, 0:2], 4, 1, far)
    on_down = remote(relay, H0.at[:, hB, 5:7], 4, 3, far)

    @pl.when(col == COLUMN - 1)
    def _():
        up_r.start()

    @pl.when(col == 0)
    def _():
        down_r.start()

    up_a.start()
    down_a.start()

    @pl.when(col != COLUMN - 1)
    def _():
        up_b.start()

    @pl.when(col != 0)
    def _():
        down_b.start()

    first = [
        remote(state.at[:, 14:16], F0.at[:, 0:2], 5, 5, at(1, 0)),
        remote(state.at[:, 0:2], F0.at[:, 18:20], 6, 6, at(-1, 0)),
        remote(state.at[:, 15:16, 15:16], H0.at[:, 1:2, 1:2], 7, 7, at(1, 1)),
        remote(state.at[:, 15:16, 0:1], H0.at[:, 1:2, 5:6], 8, 8, at(1, -1)),
        remote(state.at[:, 0:1, 15:16], H0.at[:, 18:19, 1:2], 9, 9, at(-1, 1)),
        remote(state.at[:, 0:1, 0:1], H0.at[:, 18:19, 5:6], 10, 10, at(-1, -1)),
    ]
    planes = remote(pack, packed, 11, 11, at(0, 0, -1))
    planes.start()
    for copy in first:
        copy.start()

    @pl.when(col == 2)
    def _():
        up_r.wait_recv()
        on_up.start()

    @pl.when(col == 1)
    def _():
        down_r.wait_recv()
        on_down.start()

    planes.wait_recv()
    second = [
        remote(packed.at[0:FIELDS, top], eh.at[:, 0:2], 12, 12, at(0, 1)),
        remote(packed.at[0:FIELDS, bottom], eh.at[:, 5:7], 13, 13, at(0, -1)),
        remote(packed.at[FIELDS + 1], xl, 14, 14, at(1, 0)),
        remote(packed.at[FIELDS], xr, 15, 15, at(-1, 0)),
        remote(packed.at[FIELDS + 1, 15:16], xlh.at[1:2], 16, 16, at(1, 1)),
        remote(packed.at[FIELDS + 1, 0:1], xlh.at[5:6], 17, 17, at(1, -1)),
        remote(packed.at[FIELDS, 15:16], xrh.at[1:2], 18, 18, at(-1, 1)),
        remote(packed.at[FIELDS, 0:1], xrh.at[5:6], 19, 19, at(-1, -1)),
    ]
    for copy in second:
        copy.start()

    own[3].wait()
    first_moves = jnp.full((8, 128), shifts[0], jnp.int32) == 2
    first_rows = jnp.full((256, 128), shifts[0], jnp.int32) == 2
    r24 = iota((24, 128), 0)
    offset = jnp.where(r24 < 16, r24, jnp.where(r24 <= 18, r24 - 18, r24 - 5))
    wanted = lax.rem(gy * W + offset + ny * W, ny * W)
    pick = (iota((24, 128), 1) == wanted).astype(f32)
    xrow = iota((256, 128), 0)
    wlane = iota((256, 128), 1)
    wgroup = wlane // 6
    wspot = wlane - 6 * wgroup
    same = lax.rem(gx * W - 2 + wgroup + nx * W, nx * W) == xrow
    total = jnp.zeros((24, 128), f32)
    for k in range(2):
        grid = jnp.where(first_rows, seedbuf[0, k], seedbuf[1, k]).astype(f32)
        lines = lax.dot_general(pick, grid, (((1,), (1,)), ((), ())), preferred_element_type=f32)
        spread = (same & (wspot == 2 + k)).astype(f32)
        total = total + jnp.dot(lines, spread, preferred_element_type=f32)
    marks[...] = total

    own[1].wait()
    own[2].wait()
    for copy in first:
        copy.wait()
    for copy in second:
        copy.wait()
    planes.wait_send()
    up_a.wait()
    down_a.wait()
    up_b.wait()
    down_b.wait()

    @pl.when((col == 1) | (col == 2))
    def _():
        on_up.wait_send()

    tiles = (slice(0, 8), slice(8, 16))
    last = jnp.full((8, 128), gz, jnp.int32) == nz - 1
    lowest = jnp.full((8, 128), gz, jnp.int32) == 0
    enters = (spot == 2) | (spot == 3)

    def gather_own(src, count, dst, base, lo, hi):
        def body(xi, carry):
            shift = lax.rem(6 * xi + 2, 128)
            mask = (group == xi) & (spot < 2)
            new = []
            for i in range(FIELDS * count):
                f, t = i // count, i % count
                moved = pltpu.roll(src[f, xi, 8 * t:8 * t + 8], shift, 1)
                new.append(jnp.where(mask, moved, carry[i]))
            return tuple(new)

        done = lax.fori_loop(lo, hi, body, tuple(base))
        for i in range(FIELDS * count):
            f, t = i // count, i % count
            dst[f, 8 * t:8 * t + 8] = done[i]

    def entering(f, rows):
        if f == GRAINS:
            return jnp.full((8, 128), melt_solute, f32)
        return jnp.where(marks[rows] == float(f), nucleus, 0.0)

    def received(tile, left, right, f, rows):
        tile = jnp.where(lane < 12, pltpu.roll(left, (-12 * f) % 128, 1), tile)
        tile = jnp.where((lane >= 108) & (lane < 120), pltpu.roll(right, (108 - 12 * f) % 128, 1), tile)
        edge = jnp.where(first_moves & enters, entering(f, rows), 0.0)
        return jnp.where(last, edge, tile)

    base = [received(packed[f, r], xl[r], xr[r], f, r) for f in range(FIELDS) for r in tiles]
    gather_own(F0, 2, E0m, base, 0, 20)
    halo = slice(16, 24)
    base = [received(eh[f], xlh[...], xrh[...], f, halo) for f in range(FIELDS)]
    gather_own(H0, 1, E0h, base, 1, 19)
    for f in range(FIELDS):
        E0h[f, 2:3] = E0m[f, 0:1]
        E0h[f, 4:5] = E0m[f, 15:16]

    rates = [step_rate * mob[g] for g in range(GRAINS)]
    keep = [1.0 - 6.0 * stiffness * r for r in rates]
    spreadrate = [stiffness * r for r in rates]

    def advance(c, beside, theta):
        squares = c[0] * c[0]
        for g in range(1, GRAINS):
            squares = squares + c[g] * c[g]
        s = c[GRAINS]
        well = squares - theta + coupling * s
        fresh = []
        after = None
        for g in range(GRAINS):
            new = c[g] * (keep[g] - rates[g] * well) + spreadrate[g] * beside[g]
            after = new * new if after is None else after + new * new
            fresh.append(new)
        solute = s * ((1.0 - 6.0 * diffusion) - rejection * (after - squares)) + diffusion * beside[GRAINS]
        return fresh + [solute]

    def theta_of(plane):
        return 1.0 - 2.0 * (plane.astype(f32) + 0.5) / (nz * 128.0)

    base_plane = gz * 128
    shift1 = jnp.full((8, 128), shifts[0], jnp.int32)
    theta_main = [theta_of(base_plane + lane - shift1), theta_of(base_plane + lane - 2)]
    theta_pack = [theta_of(base_plane + 126 + spot - shift1), theta_of(base_plane + 126 + spot - 2)]
    open_below = [~(lowest & first_moves & (lane == 2)), ~(lowest & (lane == 2))]
    final = lane == 127

    def rows_beside(above, tile, below, is_main):
        return jnp.where(row == 0, above, pltpu.roll(tile, 1, 0)) + jnp.where(row == 7, below, pltpu.roll(tile, 7, 0))

    def main_beside(F, H, E, f, xi, t, step):
        tile = F[f, xi, tiles[t]]
        other = F[f, xi, tiles[1 - t]]
        h = H[f, xi]
        if t == 0:
            above, below = pltpu.roll(h, 7, 0), pltpu.roll(other, 7, 0)
        else:
            above, below = pltpu.roll(other, 1, 0), pltpu.roll(h, 2, 0)
        beside = jnp.where(row == 0, above, pltpu.roll(tile, 1, 0)) + jnp.where(row == 7, below, pltpu.roll(tile, 7, 0))
        beside = beside + F[f, xi - 1, tiles[t]] + F[f, xi + 1, tiles[t]]
        nextplane = pltpu.roll(E[f, tiles[t]], 125 - 6 * xi, 1)
        beside = beside + jnp.where(open_below[step], pltpu.roll(tile, 1, 1), 0.0)
        return tile, beside + jnp.where(final, nextplane, pltpu.roll(tile, 127, 1))

    def halo_beside(f, xi):
        tile = H0[f, xi]
        beside = pltpu.roll(tile, 1, 0) + pltpu.roll(tile, 7, 0) + H0[f, xi - 1] + H0[f, xi + 1]
        nextplane = pltpu.roll(E0h[f], 125 - 6 * xi, 1)
        beside = beside + jnp.where(open_below[0], pltpu.roll(tile, 1, 1), 0.0)
        return tile, beside + jnp.where(final, nextplane, pltpu.roll(tile, 127, 1))

    def pack_beside(E, Eh, f, t):
        tile = E[f, tiles[t]]
        other = E[f, tiles[1 - t]]
        h = Eh[f]
        if t == 0:
            above, below = pltpu.roll(h, 7, 0), pltpu.roll(other, 7, 0)
        else:
            above, below = pltpu.roll(other, 1, 0), pltpu.roll(h, 2, 0)
        beside = jnp.where(row == 0, above, pltpu.roll(tile, 1, 0)) + jnp.where(row == 7, below, pltpu.roll(tile, 7, 0))
        return tile, beside + lanes_beside(tile)

    def lanes_beside(tile):
        return pltpu.roll(tile, 6, 1) + pltpu.roll(tile, 122, 1) + pltpu.roll(tile, 1, 1) + pltpu.roll(tile, 127, 1)

    def settle(new, f, rows):
        edge = jnp.where(enters, jnp.where(first_moves, new, entering(f, rows)), 0.0)
        return jnp.where(last & (spot >= 2), edge, new)

    def apply(pairs, theta):
        return advance([p[0] for p in pairs], [p[1] for p in pairs], theta)

    for t in range(2):
        new = apply([pack_beside(E0m, E0h, f, t) for f in range(FIELDS)], theta_pack[0])
        for f in range(FIELDS):
            E1m[f, tiles[t]] = settle(new[f], f, tiles[t])
    pairs = []
    for f in range(FIELDS):
        tile = E0h[f]
        pairs.append((tile, pltpu.roll(tile, 1, 0) + pltpu.roll(tile, 7, 0) + lanes_beside(tile)))
    new = apply(pairs, theta_pack[0])
    for f in range(FIELDS):
        E1h[f] = settle(new[f], f, halo)

    @pl.loop(1, 19)
    def _(xi):
        for t in range(2):
            new = apply([main_beside(F0, H0, E0m, f, xi, t, 0) for f in range(FIELDS)], theta_main[0])
            for f in range(FIELDS):
                F1[f, xi, tiles[t]] = new[f]

    @pl.loop(2, 18)
    def _(xi):
        new = apply([halo_beside(f, xi) for f in range(FIELDS)], theta_main[0])
        for f in range(FIELDS):
            H1[f, xi] = new[f]

    for t in range(2):
        new = apply([pack_beside(E1m, E1h, f, t) for f in range(FIELDS)], theta_pack[1])
        for f in range(FIELDS):
            E2m[f, tiles[t]] = new[f]

    @pl.loop(2, 18)
    def _(xi):
        for t in range(2):
            new = apply([main_beside(F1, H1, E1m, f, xi, t, 1) for f in range(FIELDS)], theta_main[1])
            for f in range(FIELDS):
                tail = pltpu.roll(E2m[f, tiles[t]], 124 - 6 * xi, 1)
                out[f, xi - 2, tiles[t]] = jnp.where(lane < 126, pltpu.roll(new[f], 126, 1), tail)


def shards(sizes, state, mobility, seeds, frame_shifts):
    V = pltpu.VMEM
    spec = pl.BlockSpec
    return pl.pallas_call(
        functools.partial(kernel, sizes),
        out_shape=jax.ShapeDtypeStruct(state.shape, f32),
        in_specs=[
            spec(memory_space=pltpu.SMEM),
            spec(memory_space=pltpu.SMEM),
            spec(memory_space=pl.ANY),
            spec(memory_space=pl.ANY),
        ],
        out_specs=spec(memory_space=pltpu.VMEM),
        scratch_shapes=[
            V((FIELDS, 20, 16, 128), f32),
            V((FIELDS, 20, 16, 128), f32),
            V((FIELDS, 20, 8, 128), f32),
            V((FIELDS, 20, 8, 128), f32),
            V((FIELDS, 8, 2, 128), f32),
            V((FIELDS + 2, 16, 128), f32),
            V((FIELDS + 2, 16, 128), f32),
            V((16, 128), f32),
            V((16, 128), f32),
            V((8, 128), f32),
            V((8, 128), f32),
            V((FIELDS, 8, 128), f32),
            V((FIELDS, 16, 128), f32),
            V((FIELDS, 8, 128), f32),
            V((FIELDS, 16, 128), f32),
            V((FIELDS, 8, 128), f32),
            V((FIELDS, 16, 128), f32),
            V((24, 128), f32),
            V(seeds.shape, jnp.int32),
            pltpu.SemaphoreType.DMA((4,)),
            pltpu.SemaphoreType.DMA((20,)),
            pltpu.SemaphoreType.DMA((20,)),
        ],
        compiler_params=pltpu.CompilerParams(collective_id=0, has_side_effects=True),
    )(mobility, frame_shifts, state, seeds)


def solution(mesh):
    sizes = tuple(mesh.shape[a] for a in ("gx", "gy", "gz"))
    placed = (P(None, "gx", "gy", "gz"), P(), P(), P())
    return jax.shard_map(
        functools.partial(shards, sizes), mesh=mesh, in_specs=placed, out_specs=P(None, "gx", "gy", "gz"), check_vma=False
    )
```

time: 159 us -> 75.5 us (0.47)
  starting transfers between devices: 115 us -> 0 us
  Pallas kernels: 0 us -> 72.9 us
  local copies, waits for them, and re-layouts: 19 us -> 2.36 us
  other arithmetic: 11.7 us -> 0 us
  waiting for transfers between devices: 10.3 us -> 0 us
  between operations: 2.9 us -> 0.01 us
    ppermute x12 -> x0, starting transfers between devices: 115 us -> none  [the longest x4 93.5 us: padded_2(): lax.ppermute(first, axis, [(b, a) for a, b in up])]
    pallas_call x0 -> x1, Pallas kernels: none -> 72.9 us  [shards(): pl.pallas_call(functools.partial(kernel, sizes), out_shape=jax.ShapeDtype...]
    ppermute x12 -> x0, waiting for transfers between devices: 10.3 us -> none  [the longest x4 5.51 us: padded_2(): lax.ppermute(last, axis, up)]
    slice x13 -> x0, local copies, waits for them, and re-layouts: 8.35 us -> none  [the longest x2 3.03 us: extended(): lax.slice_in_dim(block, block.shape[dim] - width, None, axis=dim)]
    concatenate x4 -> x0, other arithmetic: 5.14 us -> none  [the longest x2 3.65 us: frame_section(): jnp.concatenate([padded[:, :, :, :length + depth + 1], upper], axis=3)]
    ppermute x2 -> x0, local copies, waits for them, and re-layouts: 3.68 us -> none  [extended(): lax.ppermute(lax.slice_in_dim(block, block.shape[dim] - width, None, axis...]
    gather x4 -> x0, local copies, waits for them, and re-layouts: 2.35 us -> none  [entering_planes(): marks = jnp.take(jnp.take(seeds[step], rows, axis=1), cols, axis=2)]
    sub x5 -> x0, other arithmetic: 2.19 us -> none  [the longest x2 1.95 us: update(): lap = beside - 6.0 * center]
  transfers between devices with their start and end apart: 12 -> 0, of which waited for: 3 -> 0; matrix products, arithmetic and copies ran while one was open for 8% -> 0% of each run, Pallas kernels for 0% -> 0%
where the time goes in v1:
time: 75.5 us; the launch traced here: 75.3 us
  Pallas kernels  72.9 us (97%)
  local copies, waits for them, and re-layouts  2.36 us (3%)
    pallas_call x1, Pallas kernels, shards(): pl.pallas_call(functools.partial(kernel, sizes), out_shape=jax.ShapeDtype...  72.9 us
    unnamed x1, local copies, waits for them, and re-layouts  2.36 us

profile of v1, /device:TPU:6, one launch (start us, length us, event | category | flops | bytes accessed | tf_op | source)
XLA Modules:
  0.0 75.3 jit_solution(12718204571575126505)
XLA Ops:
  0.0 72.9 %shard_map.46 = f32[9,16,16,128]{3,2,1,0:T(8,128)} custom-call(f32[8]{0:T(128)} %mob.1, s32[2]{0:T(128)} %shifts.1, f32[9,16,16,128]{3,2,1,0:T(8,128)} %state.1, s32[2,2,256,128]{3,2,1,0:T(8,128)} %seeds.1), custom_call_target="tpu_custom_call" | custom-call | tf_op jit(solution)/shard_map/pallas_call | solution.py:350
  72.9 2.4 %copy.6 = f32[9,16,16,128]{3,2,1,0:T(8,128)} copy(f32[9,16,16,128]{3,2,1,0:T(8,128)} %shard_map.46) | data formatting | bytes 2359296

commit v2 on v1

v2 whole, which is shorter than its diff:
```python
import functools

import jax
import jax.numpy as jnp
from jax import lax
from jax.experimental import pallas as pl
from jax.experimental.pallas import tpu as pltpu
from jax.sharding import PartitionSpec as P

step_rate = 0.1
stiffness = 0.7
coupling = 0.5
diffusion = 0.14
rejection = 0.5
nucleus = 0.3
melt_solute = 1.0

MESH = pl.DeviceIdType.MESH
FIELDS = 9
GRAINS = 8
W = 16
COLUMN = 4
f32 = jnp.float32


def iota(shape, dim):
    return lax.broadcasted_iota(jnp.int32, shape, dim)


def kernel(sizes, mob, shifts, state, seeds, out, F0, F1, H0, H1, relay, pack, packed, xl, xr, xlh, xrh, eh,
           E0m, E0h, E1m, E1h, E2m, E2h, marks, seedbuf, local, send, recv):
    nx, ny, nz = sizes
    gx, gy, gz = lax.axis_index("gx"), lax.axis_index("gy"), lax.axis_index("gz")
    col = lax.rem(gy, COLUMN)

    def at(dx, dy, dz=0):
        return (lax.rem(gx + dx + nx, nx), lax.rem(gy + dy + ny, ny), lax.rem(gz + dz + nz, nz))

    far = at(0, jnp.where(col >= 2, 2, -2))
    around = [at(1, 0), at(-1, 0), at(0, 1), at(0, -1), at(1, 1), at(1, -1), at(-1, 1), at(-1, -1)]
    partners = around + [at(0, 0, 1), at(0, 0, -1), far]

    barrier = pltpu.get_barrier_semaphore()
    for partner in partners:
        pl.semaphore_signal(barrier, inc=1, device_id=partner, device_id_type=MESH)

    own = [
        pltpu.make_async_copy(state, F0.at[:, 2:18], local.at[0]),
        pltpu.make_async_copy(state.at[:, :, 0:2], H0.at[:, 2:18, 2:4], local.at[1]),
        pltpu.make_async_copy(state.at[:, :, 14:16], H0.at[:, 2:18, 4:6], local.at[2]),
        pltpu.make_async_copy(seeds, seedbuf, local.at[3]),
    ]
    for copy in own:
        copy.start()

    lane = iota((8, 128), 1)
    row = iota((8, 128), 0)
    group = lane // 6
    spot = lane - 6 * group
    tiles = (slice(0, 8), slice(8, 16))
    halo = slice(16, 24)

    pl.semaphore_wait(barrier, len(partners))

    def remote(src, dst, s, r, device):
        return pltpu.make_async_remote_copy(
            src_ref=src, dst_ref=dst, send_sem=send.at[s], recv_sem=recv.at[r], device_id=device, device_id_type=MESH
        )

    A, B = slice(0, 8), slice(8, 16)
    hA, hB = slice(2, 10), slice(10, 18)
    top, bottom = slice(14, 16), slice(0, 2)
    up_a = remote(state.at[:, A, top], H0.at[:, hA, 0:2], 0, 0, at(0, 1))
    up_b = remote(state.at[:, B, top], H0.at[:, hB, 0:2], 1, 1, at(0, 1))
    down_a = remote(state.at[:, A, bottom], H0.at[:, hA, 6:8], 2, 2, at(0, -1))
    down_b = remote(state.at[:, B, bottom], H0.at[:, hB, 6:8], 3, 3, at(0, -1))
    up_r = remote(state.at[:, B, top], relay, 1, 4, at(0, -1))
    down_r = remote(state.at[:, B, bottom], relay, 3, 4, at(0, 1))
    on_up = remote(relay, H0.at[:, hB, 0:2], 4, 1, far)
    on_down = remote(relay, H0.at[:, hB, 6:8], 4, 3, far)
    sides = [
        remote(state.at[:, 14:16], F0.at[:, 0:2], 5, 5, at(1, 0)),
        remote(state.at[:, 0:2], F0.at[:, 18:20], 6, 6, at(-1, 0)),
    ]
    corners = [
        remote(state.at[:, 15:16, 15:16], H0.at[:, 1:2, 1:2], 7, 7, at(1, 1)),
        remote(state.at[:, 15:16, 0:1], H0.at[:, 1:2, 6:7], 8, 8, at(1, -1)),
        remote(state.at[:, 0:1, 15:16], H0.at[:, 18:19, 1:2], 9, 9, at(-1, 1)),
        remote(state.at[:, 0:1, 0:1], H0.at[:, 18:19, 6:7], 10, 10, at(-1, -1)),
    ]
    planes = remote(pack, packed, 11, 11, at(0, 0, -1))
    early = gy < ny // 2
    up_far, down_far = col == COLUMN - 1, col == 0

    @pl.when(early)
    def _():
        for copy in sides:
            copy.start()

    @pl.when(up_far)
    def _():
        up_r.start()
        up_a.start()

    @pl.when(down_far)
    def _():
        down_r.start()
        down_a.start()

    @pl.when(~up_far)
    def _():
        up_a.start()
        up_b.start()

    @pl.when(~down_far)
    def _():
        down_a.start()
        down_b.start()

    for copy in corners:
        copy.start()

    own[0].wait()
    for f in range(FIELDS):
        for t in range(2):
            acc = jnp.zeros((8, 128), f32)
            for x in range(W):
                moved = pltpu.roll(F0[f, x + 2, tiles[t]], 6 * (x + 2) + 2, 1)
                acc = jnp.where((group == x + 2) & (spot >= 2), moved, acc)
            pack[f, tiles[t]] = acc
    for t in range(2):
        low = jnp.zeros((8, 128), f32)
        high = jnp.zeros((8, 128), f32)
        for f in range(FIELDS):
            acc = pack[f, tiles[t]]
            here = lane // 12 == f
            low = jnp.where(here, pltpu.roll(acc, (12 * f - 12) % 128, 1), low)
            high = jnp.where(here, pltpu.roll(acc, (12 * f - 96) % 128, 1), high)
        pack[FIELDS, tiles[t]] = low
        pack[FIELDS + 1, tiles[t]] = high

    own[3].wait()
    first_moves = jnp.full((8, 128), shifts[0], jnp.int32) == 2
    first_rows = jnp.full((256, 128), shifts[0], jnp.int32) == 2
    r24 = iota((24, 128), 0)
    offset = jnp.where(r24 < 16, r24, jnp.where(r24 < 20, r24 - 18, r24 - 6))
    wanted = lax.rem(gy * W + offset + ny * W, ny * W)
    pick = (iota((24, 128), 1) == wanted).astype(f32)
    xrow = iota((256, 128), 0)
    wlane = iota((256, 128), 1)
    wgroup = wlane // 6
    wspot = wlane - 6 * wgroup
    same = lax.rem(gx * W - 2 + wgroup + nx * W, nx * W) == xrow
    total = jnp.zeros((24, 128), f32)
    for k in range(2):
        grid = jnp.where(first_rows, seedbuf[0, k], seedbuf[1, k]).astype(f32)
        lines = lax.dot_general(pick, grid, (((1,), (1,)), ((), ())), preferred_element_type=f32)
        spread = (same & (wspot == 2 + k)).astype(f32)
        total = total + jnp.dot(lines, spread, preferred_element_type=f32)
    marks[...] = total

    planes.start()

    @pl.when(col == 2)
    def _():
        up_r.wait_recv()
        on_up.start()

    @pl.when(col == 1)
    def _():
        down_r.wait_recv()
        on_down.start()

    planes.wait_recv()
    second = [
        remote(packed.at[0:FIELDS, top], eh.at[:, 0:2], 12, 12, at(0, 1)),
        remote(packed.at[0:FIELDS, bottom], eh.at[:, 6:8], 13, 13, at(0, -1)),
        remote(packed.at[FIELDS + 1, 15:16], xlh.at[1:2], 16, 16, at(1, 1)),
        remote(packed.at[FIELDS + 1, 0:1], xlh.at[6:7], 17, 17, at(1, -1)),
        remote(packed.at[FIELDS, 15:16], xrh.at[1:2], 18, 18, at(-1, 1)),
        remote(packed.at[FIELDS, 0:1], xrh.at[6:7], 19, 19, at(-1, -1)),
    ]
    second_sides = [
        remote(packed.at[FIELDS + 1], xl, 14, 14, at(1, 0)),
        remote(packed.at[FIELDS], xr, 15, 15, at(-1, 0)),
    ]
    for copy in second + second_sides:
        copy.start()

    last = jnp.full((8, 128), gz, jnp.int32) == nz - 1
    lowest = jnp.full((8, 128), gz, jnp.int32) == 0
    enters = (spot == 2) | (spot == 3)
    final = lane == 127

    rates = [step_rate * mob[g] for g in range(GRAINS)]
    keep = [1.0 - 6.0 * stiffness * r for r in rates]
    spreadrate = [stiffness * r for r in rates]

    def advance(pairs, theta):
        c = [p[0] for p in pairs]
        beside = [p[1] for p in pairs]
        squares = c[0] * c[0]
        for g in range(1, GRAINS):
            squares = squares + c[g] * c[g]
        s = c[GRAINS]
        well = squares - theta + coupling * s
        fresh = []
        after = None
        for g in range(GRAINS):
            new = c[g] * (keep[g] - rates[g] * well) + spreadrate[g] * beside[g]
            after = new * new if after is None else after + new * new
            fresh.append(new)
        solute = s * ((1.0 - 6.0 * diffusion) - rejection * (after - squares)) + diffusion * beside[GRAINS]
        return fresh + [solute]

    def theta_of(plane):
        return 1.0 - 2.0 * (plane.astype(f32) + 0.5) / (nz * 128.0)

    base_plane = gz * 128
    shift1 = jnp.full((8, 128), shifts[0], jnp.int32)
    theta_main = [theta_of(base_plane + lane - shift1), theta_of(base_plane + lane - 2)]
    theta_pack = [theta_of(base_plane + 126 + spot - shift1), theta_of(base_plane + 126 + spot - 2)]
    open_below = [~(lowest & first_moves & (lane == 2)), ~(lowest & (lane == 2))]

    def entering(f, rows):
        if f == GRAINS:
            return jnp.full((8, 128), melt_solute, f32)
        return jnp.where(marks[rows] == float(f), nucleus, 0.0)

    def at_top(tile, f, rows):
        edge = jnp.where(first_moves & enters, entering(f, rows), 0.0)
        return jnp.where(last & (spot >= 2), edge, tile)

    def settle(new, f, rows):
        edge = jnp.where(enters, jnp.where(first_moves, new, entering(f, rows)), 0.0)
        return jnp.where(last & (spot >= 2), edge, new)

    def own_planes(acc, tile, xi):
        return jnp.where((group == xi) & (spot < 2), pltpu.roll(tile, (6 * xi + 2) % 128, 1), acc)

    def side_planes(tile, left, right, f):
        tile = jnp.where(lane < 12, pltpu.roll(left, (-12 * f) % 128, 1), tile)
        return jnp.where((lane >= 108) & (lane < 120), pltpu.roll(right, (108 - 12 * f) % 128, 1), tile)

    def rows_beside(F, index, t, f):
        tile = F[index + (tiles[t],)]
        other = F[index + (tiles[1 - t],)]
        if t == 0:
            return tile, pltpu.roll(tile, 1, 0) + jnp.where(row == 7, pltpu.roll(other, 7, 0), pltpu.roll(tile, 7, 0))
        return tile, jnp.where(row == 0, pltpu.roll(other, 1, 0), pltpu.roll(tile, 1, 0)) + pltpu.roll(tile, 7, 0)

    def planes_beside(tile, packed_tile, xi, step):
        nextplane = pltpu.roll(packed_tile, 125 - 6 * xi, 1)
        below = jnp.where(open_below[step], pltpu.roll(tile, 1, 1), 0.0)
        return below + jnp.where(final, nextplane, pltpu.roll(tile, 127, 1))

    def lanes_beside(tile):
        return pltpu.roll(tile, 6, 1) + pltpu.roll(tile, 122, 1) + pltpu.roll(tile, 1, 1) + pltpu.roll(tile, 127, 1)

    def main_pair(F, E, f, xi, t, step):
        tile, beside = rows_beside(F, (f, xi), t, f)
        beside = beside + F[f, xi - 1, tiles[t]] + F[f, xi + 1, tiles[t]]
        return tile, beside + planes_beside(tile, E[f, tiles[t]], xi, step)

    def pack_pair(E, f, t):
        tile, beside = rows_beside(E, (f,), t, f)
        return tile, beside + lanes_beside(tile)

    def edge_pair(H, E, f, xi, step):
        tile = H[f, xi]
        beside = pltpu.roll(tile, 1, 0) + pltpu.roll(tile, 7, 0) + H[f, xi - 1] + H[f, xi + 1]
        return tile, beside + planes_beside(tile, E[f], xi, step)

    def edge_pack_pair(E, f):
        tile = E[f]
        return tile, pltpu.roll(tile, 1, 0) + pltpu.roll(tile, 7, 0) + lanes_beside(tile)

    def pack_steps(which):
        for t in range(2):
            if which == 1:
                new = advance([pack_pair(E0m, f, t) for f in range(FIELDS)], theta_pack[0])
                for f in range(FIELDS):
                    E1m[f, tiles[t]] = settle(new[f], f, tiles[t])
            else:
                new = advance([pack_pair(E1m, f, t) for f in range(FIELDS)], theta_pack[1])
                for f in range(FIELDS):
                    E2m[f, tiles[t]] = new[f]

    def main_first(xi):
        for t in range(2):
            new = advance([main_pair(F0, E0m, f, xi, t, 0) for f in range(FIELDS)], theta_main[0])
            for f in range(FIELDS):
                F1[f, xi, tiles[t]] = new[f]

    def ended(new, packed_tile, xi):
        return pltpu.roll(jnp.where(lane < 2, pltpu.roll(packed_tile, (126 - 6 * xi) % 128, 1), new), 126, 1)

    def main_second(xi):
        for t in range(2):
            new = advance([main_pair(F1, E1m, f, xi, t, 1) for f in range(FIELDS)], theta_main[1])
            for f in range(FIELDS):
                out[f, xi - 2, tiles[t]] = ended(new[f], E2m[f, tiles[t]], xi)

    def each(lo, hi, unroll, step):
        def body(i, carry):
            step(i)
            return carry

        lax.fori_loop(lo, hi, body, 0, unroll=unroll)

    for f in range(FIELDS):
        for t in range(2):
            tile = at_top(packed[f, tiles[t]], f, tiles[t])
            for xi in range(2, 18):
                tile = own_planes(tile, F0[f, xi, tiles[t]], xi)
            E0m[f, tiles[t]] = tile
    pack_steps(1)
    pack_steps(2)
    each(3, 17, 2, main_first)
    each(4, 16, 2, main_second)

    @pl.when(~early)
    def _():
        @pl.when(up_far)
        def _():
            up_r.wait_send()
            up_a.wait_send()

        @pl.when(down_far)
        def _():
            down_r.wait_send()
            down_a.wait_send()

        @pl.when((col == 1) | (col == 2))
        def _():
            on_up.wait_send()

        for copy in sides:
            copy.start()

    for copy in own[1:3]:
        copy.wait()
    for copy in sides + second_sides:
        copy.wait_recv()
    trims = [
        pltpu.make_async_copy(F0.at[:, lo:lo + 2, y:y + 2], H0.at[:, lo:lo + 2, r:r + 2], local.at[i])
        for i, (lo, y, r) in enumerate([(0, 0, 2), (0, 14, 4), (18, 0, 2), (18, 14, 4)])
    ]
    for copy in trims:
        copy.start()
    for f in range(FIELDS):
        for t in range(2):
            tile = side_planes(E0m[f, tiles[t]], xl[tiles[t]], xr[tiles[t]], f)
            tile = at_top(tile, f, tiles[t])
            for xi in (0, 1, 18, 19):
                tile = own_planes(tile, F0[f, xi, tiles[t]], xi)
            E0m[f, tiles[t]] = tile
    pack_steps(1)
    pack_steps(2)
    for xi in (1, 2, 17, 18):
        main_first(xi)
    for xi in (2, 3, 16, 17):
        main_second(xi)
    for copy in trims:
        copy.wait()

    for copy in corners + second:
        copy.wait_recv()
    up_a.wait_recv()
    down_a.wait_recv()
    up_b.wait_recv()
    down_b.wait_recv()

    inner = (row >= 2) & (row < 6)
    for f in range(FIELDS):
        tile = side_planes(eh[f], xlh[...], xrh[...], f)
        tile = at_top(tile, f, halo)
        mid = jnp.where(row < 4, pltpu.roll(E0m[f, 0:8], 2, 0), pltpu.roll(E0m[f, 8:16], 6, 0))
        for xi in range(1, 19):
            tile = own_planes(tile, H0[f, xi], xi)
        E0h[f] = jnp.where(inner, mid, tile)

    def between(new, t0, t1):
        first = jnp.where(row < 2, pltpu.roll(new, 7, 0), pltpu.roll(t0, 1, 0))
        second = jnp.where(row < 6, pltpu.roll(t1, 7, 0), pltpu.roll(new, 1, 0))
        return jnp.where(row < 4, first, second)

    new = advance([edge_pack_pair(E0h, f) for f in range(FIELDS)], theta_pack[0])
    for f in range(FIELDS):
        E1h[f] = between(settle(new[f], f, halo), E1m[f, 0:8], E1m[f, 8:16])

    def edge_first(xi):
        new = advance([edge_pair(H0, E0h, f, xi, 0) for f in range(FIELDS)], theta_main[0])
        for f in range(FIELDS):
            H1[f, xi] = between(new[f], F1[f, xi, 0:8], F1[f, xi, 8:16])

    each(1, 19, 3, edge_first)
    new = advance([edge_pack_pair(E1h, f) for f in range(FIELDS)], theta_pack[1])
    for f in range(FIELDS):
        E2h[f] = new[f]

    def edge_second(xi):
        new = advance([edge_pair(H1, E1h, f, xi, 1) for f in range(FIELDS)], theta_main[1])
        for f in range(FIELDS):
            tile = ended(new[f], E2h[f], xi)
            out[f, xi - 2, 0:2] = tile[1:3]
            out[f, xi - 2, 14:16] = tile[5:7]

    each(2, 18, 4, edge_second)

    for copy in corners + second + second_sides + [planes]:
        copy.wait_send()

    @pl.when(early)
    def _():
        @pl.when((col == 1) | (col == 2))
        def _():
            on_up.wait_send()

        @pl.when(up_far)
        def _():
            up_r.wait_send()
            up_a.wait_send()

        @pl.when(down_far)
        def _():
            down_r.wait_send()
            down_a.wait_send()

    @pl.when(~up_far)
    def _():
        up_a.wait_send()
        up_b.wait_send()

    @pl.when(~down_far)
    def _():
        down_a.wait_send()
        down_b.wait_send()

    for copy in sides:
        copy.wait_send()


def shards(sizes, state, mobility, seeds, frame_shifts):
    V = pltpu.VMEM
    spec = pl.BlockSpec
    return pl.pallas_call(
        functools.partial(kernel, sizes),
        out_shape=jax.ShapeDtypeStruct(state.shape, f32),
        in_specs=[
            spec(memory_space=pltpu.SMEM),
            spec(memory_space=pltpu.SMEM),
            spec(memory_space=pl.ANY),
            spec(memory_space=pl.ANY),
        ],
        out_specs=spec(memory_space=pltpu.VMEM),
        scratch_shapes=[
            V((FIELDS, 20, 16, 128), f32),
            V((FIELDS, 20, 16, 128), f32),
            V((FIELDS, 20, 8, 128), f32),
            V((FIELDS, 20, 8, 128), f32),
            V((FIELDS, 8, 2, 128), f32),
            V((FIELDS + 2, 16, 128), f32),
            V((FIELDS + 2, 16, 128), f32),
            V((16, 128), f32),
            V((16, 128), f32),
            V((8, 128), f32),
            V((8, 128), f32),
            V((FIELDS, 8, 128), f32),
            V((FIELDS, 16, 128), f32),
            V((FIELDS, 8, 128), f32),
            V((FIELDS, 16, 128), f32),
            V((FIELDS, 8, 128), f32),
            V((FIELDS, 16, 128), f32),
            V((FIELDS, 8, 128), f32),
            V((24, 128), f32),
            V(seeds.shape, jnp.int32),
            pltpu.SemaphoreType.DMA((4,)),
            pltpu.SemaphoreType.DMA((20,)),
            pltpu.SemaphoreType.DMA((20,)),
        ],
        compiler_params=pltpu.CompilerParams(collective_id=0, has_side_effects=True),
    )(mobility, frame_shifts, state, seeds)


def solution(mesh):
    sizes = tuple(mesh.shape[a] for a in ("gx", "gy", "gz"))
    placed = (P(None, "gx", "gy", "gz"), P(), P(), P())
    return jax.shard_map(
        functools.partial(shards, sizes), mesh=mesh, in_specs=placed, out_specs=P(None, "gx", "gy", "gz"), check_vma=False
    )
```

time: 75.5 us -> 64 us (0.85)
  Pallas kernels: 72.9 us -> 61.5 us
    pallas_call x1, Pallas kernels: 72.9 us -> 61.5 us  [shards(): pl.pallas_call(functools.partial(kernel, sizes), out_shape=jax.ShapeDtype...]
where the time goes in v2:
time: 64 us; the launch traced here: 63.8 us
  Pallas kernels  61.5 us (96%)
  local copies, waits for them, and re-layouts  2.36 us (4%)
    pallas_call x1, Pallas kernels, shards(): pl.pallas_call(functools.partial(kernel, sizes), out_shape=jax.ShapeDtype...  61.5 us
    unnamed x1, local copies, waits for them, and re-layouts  2.36 us

profile of v2, /device:TPU:6, one launch (start us, length us, event | category | flops | bytes accessed | tf_op | source)
XLA Modules:
  0.0 63.8 jit_solution(9628109912190785146)
XLA Ops:
  0.0 61.5 %shard_map.46 = f32[9,16,16,128]{3,2,1,0:T(8,128)} custom-call(f32[8]{0:T(128)} %mob.1, s32[2]{0:T(128)} %shifts.1, f32[9,16,16,128]{3,2,1,0:T(8,128)} %state.1, s32[2,2,256,128]{3,2,1,0:T(8,128)} %seeds.1), custom_call_target="tpu_custom_call" | custom-call | tf_op jit(solution)/shard_map/pallas_call | solution.py:447
  61.5 2.4 %copy.6 = f32[9,16,16,128]{3,2,1,0:T(8,128)} copy(f32[9,16,16,128]{3,2,1,0:T(8,128)} %shard_map.46) | data formatting | bytes 2359296

commit v3 on v2

--- a/solution.py
+++ b/solution.py
@@ -28,7 +28,8 @@
 
 
 def kernel(sizes, mob, shifts, state, seeds, out, F0, F1, H0, H1, relay, pack, packed, xl, xr, xlh, xrh, eh,
-           E0m, E0h, E1m, E1h, E2m, E2h, marks, seedbuf, local, send, recv):
+           E0m, E0h, E1m, E1h, E2m, E2h, marks, seedbuf, local, send, recv,
+           far_ready, ring_ready):
     nx, ny, nz = sizes
     gx, gy, gz = lax.axis_index("gx"), lax.axis_index("gy"), lax.axis_index("gz")
     col = lax.rem(gy, COLUMN)
@@ -36,13 +37,41 @@
     def at(dx, dy, dz=0):
         return (lax.rem(gx + dx + nx, nx), lax.rem(gy + dy + ny, ny), lax.rem(gz + dz + nz, nz))
 
+    early = gy < ny // 2
     far = at(0, jnp.where(col >= 2, 2, -2))
-    around = [at(1, 0), at(-1, 0), at(0, 1), at(0, -1), at(1, 1), at(1, -1), at(-1, 1), at(-1, -1)]
-    partners = around + [at(0, 0, 1), at(0, 0, -1), far]
+    around = [(1, 0), (-1, 0), (0, 1), (0, -1), (1, 1), (1, -1), (-1, 1), (-1, -1)]
+    up_far, down_far = col == COLUMN - 1, col == 0
+    middle = (col == 1) | (col == 2)
+
+    def crosses(dy):
+        return up_far if dy == 1 else down_far
 
     barrier = pltpu.get_barrier_semaphore()
-    for partner in partners:
-        pl.semaphore_signal(barrier, inc=1, device_id=partner, device_id_type=MESH)
+
+    def tell(semaphore, device):
+        pl.semaphore_signal(semaphore, inc=1, device_id=device, device_id_type=MESH)
+
+    for dz in (1, -1):
+        tell(barrier, at(0, 0, dz))
+    for dx, dy in around:
+        silent = (gx == nx - 1) if dx == 1 else None
+        if dy:
+            cross = crosses(dy)
+            held = cross & ~early
+            if silent is not None:
+                held = held | (~cross & silent)
+        else:
+            held = silent
+        if held is None:
+            tell(barrier, at(dx, dy))
+        else:
+            @pl.when(~held)
+            def _(dx=dx, dy=dy):
+                tell(barrier, at(dx, dy))
+
+    @pl.when(early)
+    def _():
+        tell(barrier, far)
 
     own = [
         pltpu.make_async_copy(state, F0.at[:, 2:18], local.at[0]),
@@ -60,7 +89,28 @@
     tiles = (slice(0, 8), slice(8, 16))
     halo = slice(16, 24)
 
-    pl.semaphore_wait(barrier, len(partners))
+    n_far = jnp.where(middle, 1, 4)
+    n_ring = jnp.where(middle, 3, 2)
+    first_end, last_end = gx == 0, gx == nx - 1
+    n_near = 11 - n_far - jnp.where(first_end | last_end, n_ring, 0)
+    pl.semaphore_wait(barrier, n_near + jnp.where(early, 0, n_far) + jnp.where(last_end, n_ring, 0))
+
+    @pl.when(~early)
+    def _():
+        tell(far_ready, far)
+        for dy in (1, -1):
+            @pl.when(crosses(dy))
+            def _(dy=dy):
+                for dx in (-1, 0, 1):
+                    tell(far_ready, at(dx, dy))
+
+    @pl.when(last_end)
+    def _():
+        tell(ring_ready, at(1, 0))
+        for dy in (1, -1):
+            @pl.when(~crosses(dy))
+            def _(dy=dy):
+                tell(ring_ready, at(1, dy))
 
     def remote(src, dst, s, r, device):
         return pltpu.make_async_remote_copy(
@@ -89,23 +139,46 @@
         remote(state.at[:, 0:1, 0:1], H0.at[:, 18:19, 6:7], 10, 10, at(-1, -1)),
     ]
     planes = remote(pack, packed, 11, 11, at(0, 0, -1))
-    early = gy < ny // 2
-    up_far, down_far = col == COLUMN - 1, col == 0
+
+    def begin(copies, when):
+        for (dx, dy), copy in copies:
+            cross = crosses(dy) if dy else jnp.bool_(False)
+            waits_far = cross & early
+            waits_ring = (first_end & ~cross) if dx == -1 else jnp.bool_(False)
+            cond = [~waits_far & ~waits_ring, waits_ring, waits_far][when]
+
+            @pl.when(cond)
+            def _(copy=copy):
+                copy.start()
+
+    turns = [(1, 1), (1, -1), (-1, 1), (-1, -1)]
+    corners_to = list(zip(turns, corners))
+    sides_to = list(zip([(1, 0), (-1, 0)], sides))
+
+    @pl.when(up_far)
+    def _():
+        up_r.start()
+
+    @pl.when(down_far)
+    def _():
+        down_r.start()
+
+    def send_far():
+        @pl.when(up_far)
+        def _():
+            up_a.start()
+
+        @pl.when(down_far)
+        def _():
+            down_a.start()
+
+    @pl.when(~early)
+    def _():
+        send_far()
 
     @pl.when(early)
     def _():
-        for copy in sides:
-            copy.start()
-
-    @pl.when(up_far)
-    def _():
-        up_r.start()
-        up_a.start()
-
-    @pl.when(down_far)
-    def _():
-        down_r.start()
-        down_a.start()
+        begin(sides_to, 0)
 
     @pl.when(~up_far)
     def _():
@@ -117,8 +190,7 @@
         down_a.start()
         down_b.start()
 
-    for copy in corners:
-        copy.start()
+    begin(corners_to, 0)
 
     own[0].wait()
     for f in range(FIELDS):
@@ -161,15 +233,20 @@
 
     planes.start()
 
-    @pl.when(col == 2)
-    def _():
-        up_r.wait_recv()
-        on_up.start()
-
-    @pl.when(col == 1)
-    def _():
-        down_r.wait_recv()
-        on_down.start()
+    def pass_on():
+        @pl.when(col == 2)
+        def _():
+            up_r.wait_recv()
+            on_up.start()
+
+        @pl.when(col == 1)
+        def _():
+            down_r.wait_recv()
+            on_down.start()
+
+    @pl.when(~early)
+    def _():
+        pass_on()
 
     planes.wait_recv()
     second = [
@@ -184,8 +261,8 @@
         remote(packed.at[FIELDS + 1], xl, 14, 14, at(1, 0)),
         remote(packed.at[FIELDS], xr, 15, 15, at(-1, 0)),
     ]
-    for copy in second + second_sides:
-        copy.start()
+    second_to = list(zip([(0, 1), (0, -1)] + turns, second)) + list(zip([(1, 0), (-1, 0)], second_sides))
+    begin(second_to, 0)
 
     last = jnp.full((8, 128), gz, jnp.int32) == nz - 1
     lowest = jnp.full((8, 128), gz, jnp.int32) == 0
@@ -331,12 +408,26 @@
             down_r.wait_send()
             down_a.wait_send()
 
-        @pl.when((col == 1) | (col == 2))
+        @pl.when(middle)
         def _():
             on_up.wait_send()
 
-        for copy in sides:
-            copy.start()
+        begin(sides_to, 0)
+
+    @pl.when(first_end)
+    def _():
+        pl.semaphore_wait(ring_ready, n_ring)
+        begin(sides_to, 1)
+        begin(corners_to, 1)
+        begin(second_to, 1)
+
+    @pl.when(early)
+    def _():
+        pl.semaphore_wait(far_ready, n_far)
+        send_far()
+        begin(corners_to, 2)
+        begin(second_to, 2)
+        pass_on()
 
     for copy in own[1:3]:
         copy.wait()
@@ -413,7 +504,7 @@
 
     @pl.when(early)
     def _():
-        @pl.when((col == 1) | (col == 2))
+        @pl.when(middle)
         def _():
             on_up.wait_send()
 
@@ -478,6 +569,8 @@
             pltpu.SemaphoreType.DMA((4,)),
             pltpu.SemaphoreType.DMA((20,)),
             pltpu.SemaphoreType.DMA((20,)),
+            pltpu.SemaphoreType.REGULAR,
+            pltpu.SemaphoreType.REGULAR,
         ],
         compiler_params=pltpu.CompilerParams(collective_id=0, has_side_effects=True),
     )(mobility, frame_shifts, state, seeds)

time: 64 us -> 58.3 us (0.911); the launches traced: 63.8 us -> 57.3 us
  Pallas kernels: 61.5 us -> 54.9 us
    pallas_call x1, Pallas kernels: 61.5 us -> 54.9 us  [shards(): pl.pallas_call(functools.partial(kernel, sizes), out_shape=jax.ShapeDtype...]
where the time goes in v3:
time: 58.3 us; the launch traced here: 57.3 us
  Pallas kernels  54.9 us (94%)
  local copies, waits for them, and re-layouts  2.36 us (4%)
    pallas_call x1, Pallas kernels, shards(): pl.pallas_call(functools.partial(kernel, sizes), out_shape=jax.ShapeDtype...  54.9 us
    unnamed x1, local copies, waits for them, and re-layouts  2.36 us

profile of v3, /device:TPU:6, one launch (start us, length us, event | category | flops | bytes accessed | tf_op | source)
XLA Modules:
  0.0 57.3 jit_solution(6562474115277068180)
XLA Ops:
  0.0 54.9 %shard_map.46 = f32[9,16,16,128]{3,2,1,0:T(8,128)} custom-call(f32[8]{0:T(128)} %mob.1, s32[2]{0:T(128)} %shifts.1, f32[9,16,16,128]{3,2,1,0:T(8,128)} %state.1, s32[2,2,256,128]{3,2,1,0:T(8,128)} %seeds.1), custom_call_target="tpu_custom_call" | custom-call | tf_op jit(solution)/shard_map/pallas_call | solution.py:538
  54.9 2.4 %copy.6 = f32[9,16,16,128]{3,2,1,0:T(8,128)} copy(f32[9,16,16,128]{3,2,1,0:T(8,128)} %shard_map.46) | data formatting | bytes 2359296

commit v4 on v3

--- a/solution.py
+++ b/solution.py
@@ -326,27 +326,26 @@
             return tile, pltpu.roll(tile, 1, 0) + jnp.where(row == 7, pltpu.roll(other, 7, 0), pltpu.roll(tile, 7, 0))
         return tile, jnp.where(row == 0, pltpu.roll(other, 1, 0), pltpu.roll(tile, 1, 0)) + pltpu.roll(tile, 7, 0)
 
-    def planes_beside(tile, packed_tile, xi, step):
-        nextplane = pltpu.roll(packed_tile, 125 - 6 * xi, 1)
+    def planes_beside(tile, nextplane, step):
         below = jnp.where(open_below[step], pltpu.roll(tile, 1, 1), 0.0)
         return below + jnp.where(final, nextplane, pltpu.roll(tile, 127, 1))
 
     def lanes_beside(tile):
         return pltpu.roll(tile, 6, 1) + pltpu.roll(tile, 122, 1) + pltpu.roll(tile, 1, 1) + pltpu.roll(tile, 127, 1)
 
-    def main_pair(F, E, f, xi, t, step):
+    def main_pair(F, ahead, f, xi, t, step):
         tile, beside = rows_beside(F, (f, xi), t, f)
         beside = beside + F[f, xi - 1, tiles[t]] + F[f, xi + 1, tiles[t]]
-        return tile, beside + planes_beside(tile, E[f, tiles[t]], xi, step)
+        return tile, beside + planes_beside(tile, ahead[f], step)
 
     def pack_pair(E, f, t):
         tile, beside = rows_beside(E, (f,), t, f)
         return tile, beside + lanes_beside(tile)
 
-    def edge_pair(H, E, f, xi, step):
+    def edge_pair(H, ahead, f, xi, step):
         tile = H[f, xi]
         beside = pltpu.roll(tile, 1, 0) + pltpu.roll(tile, 7, 0) + H[f, xi - 1] + H[f, xi + 1]
-        return tile, beside + planes_beside(tile, E[f], xi, step)
+        return tile, beside + planes_beside(tile, ahead[f], step)
 
     def edge_pack_pair(E, f):
         tile = E[f]
@@ -361,22 +360,27 @@
             else:
                 new = advance([pack_pair(E1m, f, t) for f in range(FIELDS)], theta_pack[1])
                 for f in range(FIELDS):
-                    E2m[f, tiles[t]] = new[f]
+                    E2m[f, tiles[t]] = joined(E1m[f, tiles[t]], new[f])
 
     def main_first(xi):
         for t in range(2):
-            new = advance([main_pair(F0, E0m, f, xi, t, 0) for f in range(FIELDS)], theta_main[0])
+            ahead = [pltpu.roll(E0m[f, tiles[t]], 125 - 6 * xi, 1) for f in range(FIELDS)]
+            new = advance([main_pair(F0, ahead, f, xi, t, 0) for f in range(FIELDS)], theta_main[0])
             for f in range(FIELDS):
                 F1[f, xi, tiles[t]] = new[f]
 
-    def ended(new, packed_tile, xi):
-        return pltpu.roll(jnp.where(lane < 2, pltpu.roll(packed_tile, (126 - 6 * xi) % 128, 1), new), 126, 1)
+    def joined(first, second):
+        return jnp.where(spot == 1, pltpu.roll(first, 127, 1), second)
+
+    def ended(new, ahead):
+        return pltpu.roll(jnp.where(lane < 2, ahead, new), 126, 1)
 
     def main_second(xi):
         for t in range(2):
-            new = advance([main_pair(F1, E1m, f, xi, t, 1) for f in range(FIELDS)], theta_main[1])
+            ahead = [pltpu.roll(E2m[f, tiles[t]], 126 - 6 * xi, 1) for f in range(FIELDS)]
+            new = advance([main_pair(F1, ahead, f, xi, t, 1) for f in range(FIELDS)], theta_main[1])
             for f in range(FIELDS):
-                out[f, xi - 2, tiles[t]] = ended(new[f], E2m[f, tiles[t]], xi)
+                out[f, xi - 2, tiles[t]] = ended(new[f], ahead[f])
 
     def each(lo, hi, unroll, step):
         def body(i, carry):
@@ -481,19 +485,21 @@
         E1h[f] = between(settle(new[f], f, halo), E1m[f, 0:8], E1m[f, 8:16])
 
     def edge_first(xi):
-        new = advance([edge_pair(H0, E0h, f, xi, 0) for f in range(FIELDS)], theta_main[0])
+        ahead = [pltpu.roll(E0h[f], 125 - 6 * xi, 1) for f in range(FIELDS)]
+        new = advance([edge_pair(H0, ahead, f, xi, 0) for f in range(FIELDS)], theta_main[0])
         for f in range(FIELDS):
             H1[f, xi] = between(new[f], F1[f, xi, 0:8], F1[f, xi, 8:16])
 
     each(1, 19, 3, edge_first)
     new = advance([edge_pack_pair(E1h, f) for f in range(FIELDS)], theta_pack[1])
     for f in range(FIELDS):
-        E2h[f] = new[f]
+        E2h[f] = joined(E1h[f], new[f])
 
     def edge_second(xi):
-        new = advance([edge_pair(H1, E1h, f, xi, 1) for f in range(FIELDS)], theta_main[1])
+        ahead = [pltpu.roll(E2h[f], 126 - 6 * xi, 1) for f in range(FIELDS)]
+        new = advance([edge_pair(H1, ahead, f, xi, 1) for f in range(FIELDS)], theta_main[1])
         for f in range(FIELDS):
-            tile = ended(new[f], E2h[f], xi)
+            tile = ended(new[f], ahead[f])
             out[f, xi - 2, 0:2] = tile[1:3]
             out[f, xi - 2, 14:16] = tile[5:7]
 

time: 58.3 us -> 57.8 us (level)
  no operation moved by 1% of the time
where the time goes in v4:
time: 57.8 us; the launch traced here: 56.8 us
  Pallas kernels  54.4 us (94%)
  local copies, waits for them, and re-layouts  2.36 us (4%)
    pallas_call x1, Pallas kernels, shards(): pl.pallas_call(functools.partial(kernel, sizes), out_shape=jax.ShapeDtype...  54.4 us
    unnamed x1, local copies, waits for them, and re-layouts  2.36 us

profile of v4, /device:TPU:6, one launch (start us, length us, event | category | flops | bytes accessed | tf_op | source)
XLA Modules:
  0.0 56.8 jit_solution(5791878310323897306)
XLA Ops:
  0.0 54.4 %shard_map.46 = f32[9,16,16,128]{3,2,1,0:T(8,128)} custom-call(f32[8]{0:T(128)} %mob.1, s32[2]{0:T(128)} %shifts.1, f32[9,16,16,128]{3,2,1,0:T(8,128)} %state.1, s32[2,2,256,128]{3,2,1,0:T(8,128)} %seeds.1), custom_call_target="tpu_custom_call" | custom-call | tf_op jit(solution)/shard_map/pallas_call | solution.py:544
  54.4 2.4 %copy.6 = f32[9,16,16,128]{3,2,1,0:T(8,128)} copy(f32[9,16,16,128]{3,2,1,0:T(8,128)} %shard_map.46) | data formatting | bytes 2359296

commit v5 on v4

--- a/solution.py
+++ b/solution.py
@@ -46,6 +46,10 @@
     def crosses(dy):
         return up_far if dy == 1 else down_far
 
+    def even(dx):
+        other = lax.rem(gx + dx + nx, nx)
+        return (jnp.minimum(gx, other) >= nx // 2) & (jnp.maximum(gx, other) < nx - 1)
+
     barrier = pltpu.get_barrier_semaphore()
 
     def tell(semaphore, device):
@@ -57,7 +61,7 @@
         silent = (gx == nx - 1) if dx == 1 else None
         if dy:
             cross = crosses(dy)
-            held = cross & ~early
+            held = cross & ~early & ~even(dx)
             if silent is not None:
                 held = held | (~cross & silent)
         else:
@@ -69,7 +73,7 @@
             def _(dx=dx, dy=dy):
                 tell(barrier, at(dx, dy))
 
-    @pl.when(early)
+    @pl.when(early | even(0))
     def _():
         tell(barrier, far)
 
@@ -89,7 +93,8 @@
     tiles = (slice(0, 8), slice(8, 16))
     halo = slice(16, 24)
 
-    n_far = jnp.where(middle, 1, 4)
+    uneven = [jnp.where(even(dx), 0, 1) for dx in (-1, 0, 1)]
+    n_far = jnp.where(middle, uneven[1], uneven[0] + 2 * uneven[1] + uneven[2])
     n_ring = jnp.where(middle, 3, 2)
     first_end, last_end = gx == 0, gx == nx - 1
     n_near = 11 - n_far - jnp.where(first_end | last_end, n_ring, 0)
@@ -97,11 +102,14 @@
 
     @pl.when(~early)
     def _():
-        tell(far_ready, far)
+        @pl.when(~even(0))
+        def _():
+            tell(far_ready, far)
+
         for dy in (1, -1):
-            @pl.when(crosses(dy))
-            def _(dy=dy):
-                for dx in (-1, 0, 1):
+            for dx in (-1, 0, 1):
+                @pl.when(crosses(dy) & ~even(dx))
+                def _(dx=dx, dy=dy):
                     tell(far_ready, at(dx, dy))
 
     @pl.when(last_end)
@@ -143,7 +151,7 @@
     def begin(copies, when):
         for (dx, dy), copy in copies:
             cross = crosses(dy) if dy else jnp.bool_(False)
-            waits_far = cross & early
+            waits_far = cross & early & ~even(dx)
             waits_ring = (first_end & ~cross) if dx == -1 else jnp.bool_(False)
             cond = [~waits_far & ~waits_ring, waits_ring, waits_far][when]
 
@@ -172,6 +180,8 @@
         def _():
             down_a.start()
 
+    soon = ~early | even(0)
+
     @pl.when(~early)
     def _():
         send_far()
@@ -179,6 +189,10 @@
     @pl.when(early)
     def _():
         begin(sides_to, 0)
+
+    @pl.when(early & soon)
+    def _():
+        send_far()
 
     @pl.when(~up_far)
     def _():
@@ -244,7 +258,7 @@
             down_r.wait_recv()
             on_down.start()
 
-    @pl.when(~early)
+    @pl.when(soon)
     def _():
         pass_on()
 
@@ -427,11 +441,20 @@
 
     @pl.when(early)
     def _():
-        pl.semaphore_wait(far_ready, n_far)
-        send_far()
+        @pl.when(n_far > 0)
+        def _():
+            pl.semaphore_wait(far_ready, n_far)
+
+        @pl.when(~soon)
+        def _():
+            send_far()
+
         begin(corners_to, 2)
         begin(second_to, 2)
-        pass_on()
+
+        @pl.when(~soon)
+        def _():
+            pass_on()
 
     for copy in own[1:3]:
         copy.wait()

time: 57.8 us -> 57.6 us (level)
  no operation moved by 1% of the time
where the time goes in v5:
time: 57.6 us; the launch traced here: 56.8 us
  Pallas kernels  54.4 us (94%)
  local copies, waits for them, and re-layouts  2.36 us (4%)
    pallas_call x1, Pallas kernels, shards(): pl.pallas_call(functools.partial(kernel, sizes), out_shape=jax.ShapeDtype...  54.4 us
    unnamed x1, local copies, waits for them, and re-layouts  2.36 us

profile of v5, /device:TPU:6, one launch (start us, length us, event | category | flops | bytes accessed | tf_op | source)
XLA Modules:
  0.0 56.8 jit_solution(9554984361017383804)
XLA Ops:
  0.0 54.4 %shard_map.46 = f32[9,16,16,128]{3,2,1,0:T(8,128)} custom-call(f32[8]{0:T(128)} %mob.1, s32[2]{0:T(128)} %shifts.1, f32[9,16,16,128]{3,2,1,0:T(8,128)} %state.1, s32[2,2,256,128]{3,2,1,0:T(8,128)} %seeds.1), custom_call_target="tpu_custom_call" | custom-call | tf_op jit(solution)/shard_map/pallas_call | solution.py:567
  54.5 2.4 %copy.6 = f32[9,16,16,128]{3,2,1,0:T(8,128)} copy(f32[9,16,16,128]{3,2,1,0:T(8,128)} %shard_map.46) | data formatting | bytes 2359296
